TPU v7x, 256 devices: a whole 4x4x8 slice. The times are simulated.
256 devices in a mesh: grp: 8 (over x, core), wide: 32 (over y, z).
Axes of the slice: x: 4, y: 4, z: 8, core: 2. Of those that a mesh axis runs over, the one named last changes fastest.
Arguments:
- block_coords: int32 [6144, 3], P(('grp', 'wide')), may hold values from 0 to 511, as said below
- block_values: bfloat16 [6144, 64, 4096], P(('grp', 'wide')), may hold values from -384 to 384
- factor_b: bfloat16 [16384, 256], P('wide'), may hold values from -0.15625 to 0.15625
- factor_c: bfloat16 [16384, 256], P('wide'), may hold values from -0.15625 to 0.15625
Outputs:
- new_a: float32 [32768, 256], P(('grp', 'wide'))
Inputs may be any that keep to these rules, and one draw needn't show every extreme that they name: `block_coords`: block n lies on device n // 24 of the grp-major order. On each device: every mode-1 block-row b has (b // 2) modulo the wide size equal to the device's wide index; at most 6 of its blocks have a mode-1 block-row owned by one grp index, at most 2 have a mode-2 block-row in one wide index's shard of 8 block-rows, and at most 2 likewise for mode 3; each of the three bounds is reached on every device.
All inputs are finite; a program needn't handle non-finite values.
Results may differ from a plain program's by a relative error of at most 0.00055.
Values may be sent and summed in bfloat16 or wider, within the bound.
A program may use at most 128 MiB of HBM per device.

v0:
```python
import jax
import jax.numpy as jnp
from jax import lax
from jax.sharding import PartitionSpec as P

RI_DEV = 2


def slot_index(owner_ids, peer_count):
    one_hot = (owner_ids[:, None] == jnp.arange(peer_count, dtype=jnp.int32)[None, :]).astype(
        jnp.int32
    )
    before = jnp.cumsum(one_hot, axis=0) - one_hot
    return jnp.sum(before * one_hot, axis=1)


def request_table(flat_slot, local_row, slot_total):
    is_match = flat_slot[:, None] == jnp.arange(slot_total, dtype=jnp.int32)[None, :]
    return jnp.sum(jnp.where(is_match, local_row[:, None], 0), axis=0)


def block_partial(block_item):
    value_block, b_rows, c_rows = block_item
    block_edge = b_rows.shape[0]
    product = lax.dot_general(
        value_block, b_rows, (((0,), (0,)), ((), ())), preferred_element_type=jnp.float32
    )
    return jnp.sum(
        product.reshape(block_edge, block_edge, -1) * c_rows.astype(jnp.float32)[None], axis=1
    )


def local(block_coords, block_values, factor_b, factor_c):
    group_size = lax.axis_size("grp")
    wide_size = lax.axis_size("wide")
    block_count = block_coords.shape[0]
    block_edge = block_values.shape[1]
    cp_rank = factor_b.shape[1]
    shard_rows = factor_b.shape[0] // block_edge
    cap_wide = max(2, 2 * block_count // wide_size)
    cap_group = max(2, 2 * block_count // group_size)
    first_block = block_coords[:, 0]
    second_block = block_coords[:, 1]
    third_block = block_coords[:, 2]
    tile_width = block_edge * cp_rank
    owner_b = second_block // shard_rows
    owner_c = third_block // shard_rows
    flat_b = owner_b * cap_wide + slot_index(owner_b, wide_size)
    flat_c = owner_c * cap_wide + slot_index(owner_c, wide_size)
    slot_total = wide_size * cap_wide
    ask_table = jnp.stack(
        [
            request_table(flat_b, second_block % shard_rows, slot_total).reshape(
                wide_size, cap_wide
            ),
            request_table(flat_c, third_block % shard_rows, slot_total).reshape(
                wide_size, cap_wide
            ),
        ],
        axis=1,
    )
    asked_rows = lax.all_to_all(ask_table, "wide", split_axis=0, concat_axis=0, tiled=True)
    send_b = factor_b.reshape(shard_rows, tile_width)[asked_rows[:, 0, :]]
    send_c = factor_c.reshape(shard_rows, tile_width)[asked_rows[:, 1, :]]
    got_b, got_c = (
        lax.all_to_all(send_b, "wide", split_axis=0, concat_axis=0, tiled=True),
        lax.all_to_all(send_c, "wide", split_axis=0, concat_axis=0, tiled=True),
    )
    picked_b = got_b.reshape(slot_total, tile_width)[flat_b]
    picked_c = got_c.reshape(slot_total, tile_width)[flat_c]
    picked_b = picked_b.reshape(block_count, block_edge, cp_rank)
    picked_c = picked_c.reshape(block_count, block_edge, cp_rank)
    partials = lax.map(block_partial, (block_values, picked_b, picked_c))
    flat_partials = partials.reshape(block_count, tile_width)
    target_group = first_block // (wide_size * RI_DEV)
    local_row = first_block % RI_DEV
    slot_total = group_size * cap_group
    slot_place = target_group * cap_group + slot_index(target_group, group_size)
    placing = (jnp.arange(slot_total, dtype=jnp.int32)[:, None] == slot_place[None, :]).astype(
        jnp.float32
    )
    outgoing = jnp.dot(placing, flat_partials, precision=lax.Precision.HIGHEST)
    labels = (
        jnp.dot(placing, (local_row + 1).astype(jnp.float32), precision=lax.Precision.HIGHEST) - 1.0
    )
    arrived, arrived_labels = (
        lax.all_to_all(
            outgoing.reshape(group_size, cap_group, tile_width),
            "grp",
            split_axis=0,
            concat_axis=0,
            tiled=True,
        ),
        lax.all_to_all(
            labels.reshape(group_size, cap_group), "grp", split_axis=0, concat_axis=0, tiled=True
        ),
    )
    owner_pick = (
        arrived_labels.reshape(1, slot_total) == jnp.arange(RI_DEV, dtype=jnp.float32)[:, None]
    ).astype(jnp.float32)
    owned = jnp.dot(
        owner_pick, arrived.reshape(slot_total, tile_width), precision=lax.Precision.HIGHEST
    )
    local_gram_b = lax.dot_general(
        factor_b, factor_b, (((0,), (0,)), ((), ())), preferred_element_type=jnp.float32
    )
    local_gram_c = lax.dot_general(
        factor_c, factor_c, (((0,), (0,)), ((), ())), preferred_element_type=jnp.float32
    )
    gram_b, gram_c = lax.psum((local_gram_b, local_gram_c), "wide")
    normal_matrix = gram_b * gram_c
    chol_lower = jnp.linalg.cholesky(normal_matrix)
    mttkrp_rows = owned.reshape(RI_DEV * block_edge, cp_rank)
    solved = jax.scipy.linalg.cho_solve((chol_lower, True), mttkrp_rows.T)
    return solved.T


def solution(mesh):
    in_specs = (
        P(("grp", "wide"), None),
        P(("grp", "wide"), None, None),
        P("wide", None),
        P("wide", None),
    )
    out_specs = P(("grp", "wide"), None)
    return jax.shard_map(local, mesh=mesh, in_specs=in_specs, out_specs=out_specs, check_vma=False)
```

profile of v0, /device:TPU:1, one launch (start us, length us, event | category | flops | bytes accessed | tf_op | source)
XLA Modules:
  0.0 492.5 jit_solution(5199121058139540611)
XLA Ops:
  9.0 12.0 %all-to-all-start.1 = ((s32[32,2,2]{2,1,0:T(2,128)}), s32[32,2,2]{2,1,0:T(2,128)S(1)}, u32[]{:S(2)}, u32[]{:S(2)}) async-start(s32[32,2,2]{2,1,0:T(2,128)} %copy.43), calls=%async_computation.1 | async-start | bytes 65536 | tf_op jit(solution)/shard_map/all_to_all | solution.py:62
  21.1 1.1 reshape.172
  22.2 7.7 %all-to-all-done.1 = s32[32,2,2]{2,1,0:T(2,128)S(1)} async-done(((s32[32,2,2]{2,1,0:T(2,128)}), s32[32,2,2]{2,1,0:T(2,128)S(1)}, u32[]{:S(2)}, u32[]{:S(2)}) %all-to-all-start.1) | async-done | bytes 544 | tf_op jit(solution)/shard_map/all_to_all | solution.py:62
  30.2 1.9 gather_fusion
  32.0 2.7 reshape.202
  34.7 4.1 all-to-all-start.2
  39.3 3.2 gather_fusion.2
  42.5 4.4 reshape.218
  46.9 41.3 %all-to-all-done.2 = bf16[32,2,16384]{2,1,0:T(2,128)(2,1)S(1)} async-done(((bf16[32,2,16384]{2,1,0:T(2,128)(2,1)}), bf16[32,2,16384]{2,1,0:T(2,128)(2,1)S(1)}, u32[]{:S(2)}, u32[]{:S(2)}) %all-to-all-start.2) | async-done | bytes 2097184 | tf_op jit(solution)/shard_map/all_to_all | solution.py:66
  88.2 1.3 copy-done
  89.6 6.3 %all-to-all-start.3 = ((bf16[32,2,16384]{2,1,0:T(2,128)(2,1)}), bf16[32,2,16384]{2,1,0:T(2,128)(2,1)}, u32[]{:S(2)}, u32[]{:S(2)}) async-start(bf16[32,2,16384]{2,1,0:T(2,128)(2,1)} %reshape.218), calls=%async_computation.3 | async-start | bytes 4194304 | tf_op jit(solution)/shard_map/all_to_all | solution.py:67
  98.1 2.7 reshape.173
  102.9 42.2 %all-to-all-done.3 = bf16[32,2,16384]{2,1,0:T(2,128)(2,1)} async-done(((bf16[32,2,16384]{2,1,0:T(2,128)(2,1)}), bf16[32,2,16384]{2,1,0:T(2,128)(2,1)}, u32[]{:S(2)}, u32[]{:S(2)}) %all-to-all-start.3) | async-done | bytes 2097184 | tf_op jit(solution)/shard_map/all_to_all | solution.py:67
  145.2 6.2 %all-to-all-start = ((f32[8,1,6]{2,1,0:T(1,128)}), f32[8,1,6]{2,1,0:T(1,128)S(1)}, u32[]{:S(2)}, u32[]{:S(2)}) async-start(f32[8,1,6]{2,1,0:T(1,128)} %bitcast.15), calls=%async_computation | async-start | bytes 8192 | tf_op jit(solution)/shard_map/all_to_all | solution.py:94
  151.3 2.7 reshape.176
  155.1 1.1 copy.58
  156.2 106.0 %while.11 = (s32[]{:T(128)}, f32[24,64,256]{2,1,0:T(8,128)}, bf16[24,64,4096]{2,1,0:T(8,128)(2,1)}, bf16[24,64,256]{2,1,0:T(8,128)(2,1)}, bf16[24,64,256]{2,1,0:T(8,128)(2,1)}, /*index=5*/s32[]{:T(128)}) while((s32[]{:T(128)}, f32[24,64,256]{2,1,0:T(8,128)}, bf16[24,64,4096]{2,1,0:T(8,128)(2,1)}, bf16[24,64,256]{2,1,0:T(8,128)(2,1)}, ...), condition=%wide.region_16.17_spmd, body=%wide.region_14.16_spmd.sunk | while | flops 136314880 | bytes 3014749 | solution.py:73
  156.2 1.1 constant_dynamic-slice_fusion.4
  158.5 1.4 multiply_reduce_fusion.2
  160.6 1.1 constant_dynamic-slice_fusion.4
  163.0 1.4 multiply_reduce_fusion.2
  165.0 1.1 constant_dynamic-slice_fusion.4
  167.4 1.4 multiply_reduce_fusion.2
  169.5 1.1 constant_dynamic-slice_fusion.4
  171.8 1.5 multiply_reduce_fusion.2
  173.9 1.1 constant_dynamic-slice_fusion.4
  176.2 1.4 multiply_reduce_fusion.2
  178.3 1.1 constant_dynamic-slice_fusion.4
  180.6 1.5 multiply_reduce_fusion.2
  182.7 1.1 constant_dynamic-slice_fusion.4
  185.0 1.5 multiply_reduce_fusion.2
  187.1 1.1 constant_dynamic-slice_fusion.4
  189.5 1.5 multiply_reduce_fusion.2
  191.6 1.1 constant_dynamic-slice_fusion.4
  193.9 1.4 multiply_reduce_fusion.2
  198.3 1.4 multiply_reduce_fusion.2
  202.7 1.4 multiply_reduce_fusion.2
  207.1 1.4 multiply_reduce_fusion.2
  211.5 1.5 multiply_reduce_fusion.2
  216.0 1.4 multiply_reduce_fusion.2
  220.4 1.4 multiply_reduce_fusion.2
  224.8 1.4 multiply_reduce_fusion.2
  229.2 1.5 multiply_reduce_fusion.2
  233.6 1.4 multiply_reduce_fusion.2
  235.7 1.1 constant_dynamic-slice_fusion.4
  238.0 1.4 multiply_reduce_fusion.2
  242.4 1.5 multiply_reduce_fusion.2
  246.9 1.5 multiply_reduce_fusion.2
  251.3 1.5 multiply_reduce_fusion.2
  255.7 1.5 multiply_reduce_fusion.2
  260.1 1.4 multiply_reduce_fusion.2
  262.2 1.6 reshape.238
  263.8 4.1 fusion.15
  267.9 4.8 all-to-all-start.4
  275.0 142.2 %all-reduce.4.cloned.1.call-done = (f32[256,256]{0,1:T(8,128)}, f32[256,256]{0,1:T(8,128)}) async-done(((f32[256,256]{0,1:T(8,128)}, f32[256,256]{0,1:T(8,128)}), (f32[256,256]{0,1:T(8,128)}, f32[256,256]{0,1:T(8,128)})) %all-reduce.4.cloned.1.call-update) | async-done | bytes 524304 | tf_op jit(solution)/shard_map/psum | solution.py:110
  418.5 11.7 %cholesky.50 = f32[128,128]{1,0:T(8,128)S(1)} custom-call(f32[128,128]{1,0:T(8,128)S(1)} %cholesky.118), custom_call_target="Cholesky" | custom-call | tf_op jit(solution)/shard_map/jit(cholesky)/cholesky | solution.py:112
  430.2 9.8 %custom-call.18 = f32[1,128,128]{1,2,0:T(8,128)S(1)} custom-call(f32[1,128,128]{2,1,0:T(8,128)S(1)} %get-tuple-element.90), custom_call_target="InvertDiagBlocksLowerTriangular" | custom-call | tf_op jit(solution)/shard_map/jit(cholesky)/cholesky | solution.py:112
  440.5 11.7 %cholesky.105 = f32[128,128]{1,0:T(8,128)S(1)} custom-call(f32[128,128]{1,0:T(8,128)S(1)} %convolution_subtract_fusion.2), custom_call_target="Cholesky" | custom-call | tf_op jit(solution)/shard_map/jit(cholesky)/cholesky | solution.py:112
  454.2 4.0 while.12
  455.0 1.3 bitcast_dynamic-update-slice_fusion.5
  456.9 1.3 bitcast_dynamic-update-slice_fusion.5
  458.3 19.7 %custom-call.19 = f32[2,128,128]{1,2,0:T(8,128)S(1)} custom-call(f32[2,128,128]{2,1,0:T(8,128)S(1)} %get-tuple-element.40), custom_call_target="InvertDiagBlocksLowerTriangular" | custom-call | tf_op jit(solution)/shard_map/jit(_cho_solve)/triangular_solve | solution.py:114
  478.0 2.5 reshape.179
  480.4 1.9 fusion.21
  (171 shorter events, 77.9 us)
Async XLA Ops:
  9.0 20.8 %all-to-all-start.1 = ((s32[32,2,2]{2,1,0:T(2,128)}), s32[32,2,2]{2,1,0:T(2,128)S(1)}, u32[]{:S(2)}, u32[]{:S(2)}) async-start(s32[32,2,2]{2,1,0:T(2,128)} %copy.43), calls=%async_computation.1 | async-start | bytes 65536 | tf_op jit(solution)/shard_map/all_to_all | solution.py:62
  34.7 4.2 copy-start.2
  34.7 53.5 %all-to-all-start.2 = ((bf16[32,2,16384]{2,1,0:T(2,128)(2,1)}), bf16[32,2,16384]{2,1,0:T(2,128)(2,1)S(1)}, u32[]{:S(2)}, u32[]{:S(2)}) async-start(bf16[32,2,16384]{2,1,0:T(2,128)(2,1)} %reshape.202), calls=%async_computation.2 | async-start | bytes 4194304 | tf_op jit(solution)/shard_map/all_to_all | solution.py:66
  46.9 49.2 %copy-start.3 = (s32[24,3]{0,1:T(4,128)S(1)}, s32[24,3]{0,1:T(4,128)}, u32[]{:S(2)}) copy-start(s32[24,3]{0,1:T(4,128)} %param.6) | copy-start | bytes 868
  46.9 50.2 %copy-start.1 = (bf16[512,256]{1,0:T(8,128)(2,1)S(1)}, bf16[512,256]{1,0:T(8,128)(2,1)}, u32[]{:S(2)}) copy-start(bf16[512,256]{1,0:T(8,128)(2,1)} %param.8) | copy-start | bytes 786436
  88.2 1.3 copy-start
  89.6 55.6 %all-to-all-start.3 = ((bf16[32,2,16384]{2,1,0:T(2,128)(2,1)}), bf16[32,2,16384]{2,1,0:T(2,128)(2,1)}, u32[]{:S(2)}, u32[]{:S(2)}) async-start(bf16[32,2,16384]{2,1,0:T(2,128)(2,1)} %reshape.218), calls=%async_computation.3 | async-start | bytes 4194304 | tf_op jit(solution)/shard_map/all_to_all | solution.py:67
  145.2 122.7 %all-to-all-start = ((f32[8,1,6]{2,1,0:T(1,128)}), f32[8,1,6]{2,1,0:T(1,128)S(1)}, u32[]{:S(2)}, u32[]{:S(2)}) async-start(f32[8,1,6]{2,1,0:T(1,128)} %bitcast.15), calls=%async_computation | async-start | bytes 8192 | tf_op jit(solution)/shard_map/all_to_all | solution.py:94
  267.9 210.1 %all-to-all-start.4 = ((f32[8,6,16384]{2,1,0:T(8,128)}), f32[8,6,16384]{2,1,0:T(8,128)}, u32[]{:S(2)}, u32[]{:S(2)}) async-start(f32[8,6,16384]{2,1,0:T(8,128)} %fusion.15), calls=%async_computation.4 | async-start | bytes 8388608 | tf_op jit(solution)/shard_map/all_to_all | solution.py:87
  272.7 144.5 %all-reduce.4.cloned.1.call-start = ((), (), s32[]{:S(2)}) async-start(), calls=%async_computation.5 | async-start | bytes 1048576 | tf_op jit(solution)/shard_map/psum | solution.py:110
Sparse Core Ops, SparseCore 0:
  276.9 140.2 all-reduce.3
where the time goes:
time: 501 us; the launch traced here: 493 us
  waiting for transfers between devices  233 us (47%)
  local copies, waits for them, and re-layouts  89.3 us (18%)
  other arithmetic  76 us (15%)
  matrix products  44.8 us (9%)
  starting transfers between devices  33.4 us (7%)
  between operations  15 us (3%)
    psum x1, waiting for transfers between devices, local(): gram_b, gram_c = lax.psum((local_gram_b, local_gram_c), 'wide')  142 us
    all_to_all x1, waiting for transfers between devices, local(): lax.all_to_all(send_c, 'wide', split_axis=0, concat_axis=0, tiled=True)  42.2 us
    all_to_all x1, waiting for transfers between devices, local(): lax.all_to_all(send_b, 'wide', split_axis=0, concat_axis=0, tiled=True)  41.3 us
    dynamic_slice x48, local copies, waits for them, and re-layouts, local(): partials = lax.map(block_partial, (block_values, picked_b, picked_c))  37.2 us
    dot_general x24, matrix products, block_partial(): lax.dot_general(value_block, b_rows, (((0,), (0,)), ((), ())), preferred_...  34.8 us
    another operation x6, other arithmetic, local(): chol_lower = jnp.linalg.cholesky(normal_matrix)  33.9 us
    another operation x3, other arithmetic, local(): solved = jax.scipy.linalg.cho_solve((chol_lower, True), mttkrp_rows.T)  19.7 us
    mul x24, other arithmetic, block_partial(): product.reshape(block_edge, block_edge, -1)  18.5 us
  transfers between devices with their start and end apart: 6, of which 4 were waited for; matrix products, arithmetic and copies ran while one was open for 39% of the time, Pallas kernels for 0%

commit v1 on v0

v1 whole, which is shorter than its diff:
```python
import functools, heapq
import jax, jax.numpy as jnp
from jax import lax
from jax.experimental import pallas as pl
from jax.experimental.pallas import tpu as pltpu
from jax.sharding import PartitionSpec as P

MESH = pl.DeviceIdType.MESH
BS, R = 64, 256
SHARD = 512
Q = 48
Z_AT, Z_ROWS = 4 * Q, 160
Y_AT, Y_ROWS = 4 * Q + 160, 160


def plan():
    msgs = []

    def add(name, dim, sign, src, dst, rows, deps, nbytes):
        landed = ("x", rows[1] + sign) + rows[2:] if dim == "x" else rows
        msgs.append(dict(name=name, dim=dim, sign=sign, src=src, dst=dst, rows=rows, landed=landed, deps=deps, bytes=nbytes))
        return len(msgs) - 1

    def half(sign, at, rows):
        first = (rows // 2 + 15) // 16 * 16
        return (at, first) if sign > 0 else (at + first, rows - first)

    def z_ring(tag, rows_of, pys, first_deps, count):
        ids = {}
        for d in (1, 2, 3, 4):
            for s in (1, -1):
                src = 3 + s * (d - 1)
                dst = 3 + s * d if d < 4 else 7
                rows = rows_of(None) if d < 4 else rows_of(s)
                deps = [ids[d - 1, s]] if d > 1 else list(first_deps)
                ids[d, s] = add((tag, d, s), "z", s, (pys, (src, 1)), (pys, (dst, 1)), rows, deps, count * rows[-1] * 512)
        return ids

    def at_pz(ids, pz):
        dz = pz - 3
        if dz == 0:
            return []
        return [ids[4, 1], ids[4, -1]] if dz == 4 else [ids[abs(dz), 1 if dz > 0 else -1]]

    def y_ring(tag, rows_of, pz, deps, count):
        ids = {}
        for t in (1, -1):
            rows = rows_of(None)
            ids[1, t] = add((tag, 1, t), "y", t, ((1, 1), pz), ((1 + t, 1), pz), rows, list(deps), count * rows[-1] * 512)
        for t in (1, -1):
            rows = rows_of(t)
            ids[2, t] = add((tag, 2, t), "y", t, ((1 + t, 1), pz), ((3, 1), pz), rows, [ids[1, t]], count * rows[-1] * 512)
        return ids

    def x_rows(dx, sign):
        return ("x", dx) + ((0, Q) if sign is None else half(sign, 0, Q))

    def fixed(at, rows):
        return lambda sign: ("r",) + ((at, rows) if sign is None else half(sign, at, rows))

    xz = z_ring("xz", lambda s: x_rows(0, s), (1, 1), [], 1)
    zz = z_ring("zz", fixed(Z_AT, Z_ROWS), (1, 1), [], 1)
    yy = y_ring("yy", fixed(Y_AT, Y_ROWS), (3, 1), [], 1)
    xy = y_ring("xy", lambda s: x_rows(0, s), (0, 8), list(xz.values()), 8)
    x_groups = [
        (1, (2, 3), [xz[1, 1], xz[1, -1]]),
        (1, (0, 2), [xz[2, -1], xz[3, -1]]),
        (1, (5, 3), [xz[2, 1], xz[3, 1], xz[4, 1], xz[4, -1]]),
        (2, (0, 8), [xy[1, 1]]), (0, (0, 8), [xy[1, -1]]), (3, (0, 8), [xy[2, 1], xy[2, -1]])]
    for py, pz, deps in x_groups:
        place = ((py, 1), pz)
        first = {}
        for u in (1, -1):
            rows = x_rows(0, None)
            first[u] = add(("xx", py, pz, 1, u), "x", u, place, place, rows, list(deps), pz[1] * Q * 512)
        for u in (1, -1):
            rows = x_rows(u, u)
            add(("xx", py, pz, 2, u), "x", u, place, place, rows, [first[u]], pz[1] * rows[-1] * 512)
    for pz in (3, 4, 2, 5, 1, 6, 0, 7):
        y_ring(("zy", pz), fixed(Z_AT, Z_ROWS), (pz, 1), at_pz(zz, pz), 1)
    z_ring("yzA", fixed(Y_AT, Y_ROWS), (0, 2), [yy[1, -1]], 2)
    z_ring("yzB", fixed(Y_AT, Y_ROWS), (2, 2), [yy[1, 1], yy[2, 1], yy[2, -1]], 2)
    late = {("zz", 2): [xz[2, 1], xz[2, -1]], ("zz", 3): [xz[3, 1], xz[3, -1]], ("yzA", 1): [xz[4, 1], xz[4, -1]],
            ("yzB", 1): [xz[4, 1], xz[4, -1]]}
    for m in msgs:
        m["deps"] += late.get(m["name"][:2], [])
        if m["name"][0] in (("zy", 5), ("zy", 1)) and m["name"][1] == 1:
            m["deps"] += list(xz.values())
    return msgs


def order(msgs, rate=45e3, latency=1.5):
    free = {}
    got = set()
    started = set()
    heap = []
    t_end = {}

    def issue(now):
        for i, m in enumerate(msgs):
            if i not in started and all(d in got for d in m["deps"]):
                started.add(i)
                link = (m["dim"], m["sign"])
                begin = max(now, free.get(link, 0.0))
                free[link] = begin + m["bytes"] / rate
                heapq.heappush(heap, (free[link] + latency, i))

    issue(0.0)
    seq = []
    while heap:
        t, i = heapq.heappop(heap)
        got.add(i)
        seq.append(i)
        t_end[i] = t
        issue(t)
    return seq, t_end, free


def kernel(msgs, seq, gram, b_hbm, c_hbm, full, nm, mine, g, gsib, own_sem, send, recv, sib_send, sib_recv, loc, gs, gr):
    grp, wide = lax.axis_index("grp"), lax.axis_index("wide")
    x, core = grp // 2, grp % 2
    y, z = wide // 8, wide % 8
    sib = (grp + 1 - 2 * core, wide)

    def dev(dim, s):
        if dim == "x":
            return (((x + s + 4) % 4) * 2 + core, wide)
        if dim == "y":
            return (grp, ((y + s + 4) % 4) * 8 + z)
        return (grp, y * 8 + (z + s + 8) % 8)

    def row_slice(rows):
        if rows[0] == "r":
            return pl.ds(rows[1], rows[2])
        at = ((x - rows[1] + 4) % 4) * Q + rows[2]
        return pl.ds(pl.multiple_of(at, 16), rows[3])

    def region(ref, place, rows):
        (py, npy), (pz, npz) = place
        return ref.at[pl.ds(py, npy), pl.ds(pz, npz), row_slice(rows), :]

    peers = [dev(d, s) for d in "xyz" for s in (1, -1)] + [sib]
    bar = pltpu.get_barrier_semaphore()
    for p in peers:
        pl.semaphore_signal(bar, inc=1, device_id=p, device_id_type=MESH)

    own_rows = [("x", 0, 0, Q), ("r", Z_AT, SHARD - Z_AT)]
    own_place = ((1, 1), (3, 1))
    for k, src in enumerate((b_hbm, c_hbm)):
        @pl.when(core == k)
        def _():
            for j, rows in enumerate(own_rows):
                pltpu.make_async_copy(src.at[row_slice(rows), :], mine.at[1, 3, row_slice(rows), :], own_sem.at[j]).start()
    for j, rows in enumerate(own_rows):
        pltpu.make_async_copy(b_hbm.at[row_slice(rows), :], mine.at[1, 3, row_slice(rows), :], own_sem.at[j]).wait()
    pl.semaphore_wait(bar, len(peers))

    def copy(i):
        m = msgs[i]
        return pltpu.make_async_remote_copy(
            src_ref=region(mine, m["src"], m["rows"]),
            dst_ref=region(mine, m["dst"], m["rows"]),
            send_sem=send.at[i], recv_sem=recv.at[i], device_id=dev(m["dim"], m["sign"]), device_id_type=MESH)

    def publish(place, rows):
        pltpu.make_async_remote_copy(
            src_ref=region(mine, place, rows), dst_ref=region(full.at[core], place, rows),
            send_sem=sib_send, recv_sem=sib_recv, device_id=sib, device_id_type=MESH).start()
        pltpu.make_async_copy(region(mine, place, rows), region(full.at[core], place, rows), loc).start()

    def add_gram(place, rows):
        if not gram:
            return
        (py, npy), (pz, npz) = place
        f = mine[pl.ds(py, npy), pl.ds(pz, npz), row_slice(rows), :]
        f = f.reshape(-1, R)
        g[...] += lax.dot_general(f, f, (((0,), (0,)), ((), ())), preferred_element_type=jnp.float32)

    started, got = set(), set()

    def issue():
        for i, m in enumerate(msgs):
            if i not in started and all(d in got for d in m["deps"]):
                started.add(i)
                copy(i).start()

    g[...] = jnp.zeros_like(g)
    issue()
    for rows in own_rows:
        publish(own_place, rows)
        add_gram(own_place, rows)
    for i in seq:
        copy(i).wait_recv()
        got.add(i)
        issue()
        publish(msgs[i]["dst"], msgs[i]["landed"])
        add_gram(msgs[i]["dst"], msgs[i]["landed"])
    swap = pltpu.make_async_remote_copy(src_ref=g, dst_ref=gsib, send_sem=gs, recv_sem=gr, device_id=sib, device_id_type=MESH)
    swap.start()
    for i in range(len(msgs)):
        copy(i).wait_send()
    swap.wait()
    nm[...] = g[...] * gsib[...]
    whole = pltpu.make_async_remote_copy(src_ref=mine, dst_ref=full.at[1 - core], send_sem=sib_send, recv_sem=sib_recv, device_id=sib, device_id_type=MESH)
    whole.wait()
    pltpu.make_async_copy(mine, full.at[core], loc).wait()


def gather(b, c, gram=True):
    msgs = plan()
    seq, _, _ = order(msgs)
    n = len(msgs)
    return pl.pallas_call(
        functools.partial(kernel, msgs, seq, gram),
        out_shape=(jax.ShapeDtypeStruct((2, 4, 8, SHARD, R), jnp.bfloat16), jax.ShapeDtypeStruct((R, R), jnp.float32)),
        in_specs=[pl.BlockSpec(memory_space=pl.ANY)] * 2,
        out_specs=(pl.BlockSpec(memory_space=pl.ANY), pl.BlockSpec(memory_space=pltpu.VMEM)),
        scratch_shapes=[
            pltpu.VMEM((4, 8, SHARD, R), jnp.bfloat16), pltpu.VMEM((R, R), jnp.float32), pltpu.VMEM((R, R), jnp.float32),
            pltpu.SemaphoreType.DMA((2,)), pltpu.SemaphoreType.DMA((n,)), pltpu.SemaphoreType.DMA((n,)),
            pltpu.SemaphoreType.DMA, pltpu.SemaphoreType.DMA, pltpu.SemaphoreType.DMA,
            pltpu.SemaphoreType.DMA, pltpu.SemaphoreType.DMA],
        compiler_params=pltpu.CompilerParams(collective_id=0, has_side_effects=True, vmem_limit_bytes=48 << 20),
        name="gather_factors",
    )(b, c)


NB = 64
HI = lax.Precision.HIGHEST


def sweep(m_ref, k, nb=NB):
    n = m_ref.shape[0]
    at = k * nb
    panel = m_ref[at:at + nb, :]
    r = panel
    lane = lax.broadcasted_iota(jnp.int32, (1, n), 1)
    row = lax.broadcasted_iota(jnp.int32, (nb, 1), 0)
    for j in range(nb):
        col = panel[:, at + j:at + j + 1]
        pivot = panel[j:j + 1, :]
        inv = 1.0 / col[j:j + 1, :]
        scaled = jnp.where(lane == at + j, inv, pivot * inv)
        cleared = jnp.where(lane == at + j, 0.0, panel)
        panel = jnp.where(row == j, scaled, cleared - col * scaled)
    inside = (lane >= at) & (lane < at + nb)
    w = jnp.where(inside, -panel, panel)
    m = m_ref[...]
    upd = lax.dot_general(r, w, (((0,), (0,)), ((), ())), precision=HI, preferred_element_type=jnp.float32)
    m_ref[...] = jnp.where(inside, 0.0, m) - upd
    m_ref[at:at + nb, :] = w


def block_body(chunk, where, v_ref, b_ref, c_ref, acc_ref):
    n = pl.program_id(0)

    @pl.when(n == 0)
    def _():
        acc_ref[...] = jnp.zeros_like(acc_ref)

    slot = where[n, 0]
    b = b_ref[0, 0, 0]
    c = c_ref[0, 0, 0].astype(jnp.float32)
    per = chunk // BS
    for q in range(BS // per):
        prod = lax.dot_general(v_ref[0, :, q * chunk:(q + 1) * chunk], b, (((0,), (0,)), ((), ())),
                               preferred_element_type=jnp.float32)
        acc_ref[slot, q * per:(q + 1) * per, :] += jnp.sum(prod.reshape(per, BS, R) * c[None], axis=1)


def block_sums(where, values, full):
    count = values.shape[0]

    def rows(m, col):
        return lambda n, s: (m, s[n, col], s[n, col + 1], s[n, col + 2], 0)

    grid_spec = pltpu.PrefetchScalarGridSpec(
        num_scalar_prefetch=1, grid=(count,),
        in_specs=[pl.BlockSpec((1, BS, BS * BS), lambda n, s: (n, 0, 0)),
                  pl.BlockSpec((1, 1, 1, BS, R), rows(0, 1)),
                  pl.BlockSpec((1, 1, 1, BS, R), rows(1, 4))],
        out_specs=pl.BlockSpec((16, BS, R), lambda n, s: (0, 0, 0)))
    return pl.pallas_call(
        functools.partial(block_body, 512), out_shape=jax.ShapeDtypeStruct((16, BS, R), jnp.float32),
        grid_spec=grid_spec, compiler_params=pltpu.CompilerParams(vmem_limit_bytes=40 << 20), name="block_sums",
    )(where, values, full, full)


def owner_body(acc, nm, out, m, pair, mine, parts, s1, r1, s2, r2):
    grp, wide = lax.axis_index("grp"), lax.axis_index("wide")
    x, core = grp // 2, grp % 2
    sib = (grp + 1 - 2 * core, wide)
    far = [(((x + d) % 4) * 2 + core, wide) for d in (1, 2, 3)]
    bar = pltpu.get_barrier_semaphore()
    for p in far + [sib]:
        pl.semaphore_signal(bar, inc=1, device_id=p, device_id_type=MESH)
    pl.semaphore_wait(bar, 4)
    swap = pltpu.make_async_remote_copy(src_ref=acc.at[:, 1 - core], dst_ref=pair, send_sem=s1, recv_sem=r1,
                                        device_id=sib, device_id_type=MESH)
    swap.start()
    m[...] = nm[...]
    blocks = R // NB
    sweep(m, 0)
    swap.wait()
    mine[...] = acc[:, core] + pair[...]
    copies = []
    for d in (2, 1, 3):
        copies.append(pltpu.make_async_remote_copy(
            src_ref=mine.at[(x + d) % 4], dst_ref=parts.at[d - 1], send_sem=s2.at[d - 1], recv_sem=r2.at[d - 1],
            device_id=far[d - 1], device_id_type=MESH))
        copies[-1].start()
    for k in range(1, blocks):
        sweep(m, k)
    for copy in copies:
        copy.wait()
    rows = mine[x] + parts[0] + parts[1] + parts[2]
    out[...] = -jnp.dot(rows, m[...], precision=HI, preferred_element_type=jnp.float32)


def owner_rows(acc, nm):
    rows = 2 * BS
    vmem = pl.BlockSpec(memory_space=pltpu.VMEM)
    return pl.pallas_call(
        owner_body, out_shape=jax.ShapeDtypeStruct((rows, R), jnp.float32), in_specs=[vmem, vmem], out_specs=vmem,
        scratch_shapes=[
            pltpu.VMEM((R, R), jnp.float32), pltpu.VMEM((4, rows, R), jnp.float32), pltpu.VMEM((4, rows, R), jnp.float32),
            pltpu.VMEM((3, rows, R), jnp.float32), pltpu.SemaphoreType.DMA, pltpu.SemaphoreType.DMA,
            pltpu.SemaphoreType.DMA((3,)), pltpu.SemaphoreType.DMA((3,))],
        compiler_params=pltpu.CompilerParams(collective_id=1, has_side_effects=True, vmem_limit_bytes=32 << 20),
        name="owner_rows",
    )(acc.reshape(4, 2, rows, R), nm)


def local(block_coords, block_values, factor_b, factor_c):
    wide = lax.axis_index("wide")
    y, z = wide // 8, wide % 8
    first, second, third = block_coords[:, 0], block_coords[:, 1], block_coords[:, 2]

    def place(rows):
        owner = rows // 8
        return [(y - owner // 8 + 1) % 4, (z - owner % 8 + 3) % 8, rows % 8]

    where = jnp.stack([first // 64 * 2 + first % 2] + place(second) + place(third), axis=1)
    full, nm = gather(factor_b, factor_c)
    acc = block_sums(where, block_values, full)
    return owner_rows(acc, nm)


def solution(mesh):
    in_specs = (P(("grp", "wide"), None), P(("grp", "wide"), None, None), P("wide", None), P("wide", None))
    return jax.shard_map(local, mesh=mesh, in_specs=in_specs, out_specs=P(("grp", "wide"), None), check_vma=False)
```

time: 501 us -> 125 us (0.25); the launches traced: 493 us -> 123 us
  waiting for transfers between devices: 233 us -> 0 us
  Pallas kernels: 0 us -> 114 us
  local copies, waits for them, and re-layouts: 89.3 us -> 7.24 us
  other arithmetic: 76 us -> 2.23 us
  matrix products: 44.8 us -> 0 us
  starting transfers between devices: 33.4 us -> 0 us
  between operations: 15 us -> 0.04 us
    psum x1 -> x0, waiting for transfers between devices: 142 us -> none  [local(): gram_b, gram_c = lax.psum((local_gram_b, local_gram_c), 'wide')]
    pallas_call x0 -> x3, Pallas kernels: none -> 114 us  [the longest x1 59 us: gather(): pl.pallas_call(functools.partial(kernel, msgs, seq, gram), out_shape=(jax...]
    all_to_all x5 -> x0, waiting for transfers between devices: 91.2 us -> none  [the longest x1 42.2 us: local(): lax.all_to_all(send_c, 'wide', split_axis=0, concat_axis=0, tiled=True)]
    another operation x13 -> x0, other arithmetic: 53.8 us -> none  [the longest x6 33.9 us: local(): chol_lower = jnp.linalg.cholesky(normal_matrix)]
    dot_general x29 -> x0, matrix products: 42.8 us -> none  [the longest x24 34.8 us: block_partial(): lax.dot_general(value_block, b_rows, (((0,), (0,)), ((), ())), preferred_...]
    dynamic_slice x48 -> x0, local copies, waits for them, and re-layouts: 37.2 us -> none  [local(): partials = lax.map(block_partial, (block_values, picked_b, picked_c))]
    all_to_all x5 -> x0, starting transfers between devices: 33.4 us -> none  [the longest x1 12 us: local(): lax.all_to_all(ask_table, 'wide', split_axis=0, concat_axis=0, tiled=True)]
    mul x25 -> x0, other arithmetic: 19.6 us -> none  [the longest x24 18.5 us: block_partial(): product.reshape(block_edge, block_edge, -1)]
  transfers between devices with their start and end apart: 6 -> 0, of which waited for: 4 -> 0; matrix products, arithmetic and copies ran while one was open for 39% -> 0% of each run, Pallas kernels for 0% -> 0%
where the time goes in v1:
time: 125 us; the launch traced here: 123 us
  Pallas kernels  114 us (91%)
  local copies, waits for them, and re-layouts  7.24 us (6%)
  other arithmetic  2.23 us (2%)
    pallas_call x1, Pallas kernels, gather(): pl.pallas_call(functools.partial(kernel, msgs, seq, gram), out_shape=(jax...  59 us
    pallas_call x1, Pallas kernels, owner_rows(): pl.pallas_call(owner_body, out_shape=jax.ShapeDtypeStruct((rows, R), jnp....  33.8 us
    pallas_call x1, Pallas kernels, block_sums(): pl.pallas_call(functools.partial(block_body, 512), out_shape=jax.ShapeDty...  21.1 us
    unnamed x7, local copies, waits for them, and re-layouts  7.13 us

profile of v1, /device:TPU:1, one launch (start us, length us, event | category | flops | bytes accessed | tf_op | source)
XLA Modules:
  0.0 123.4 jit_solution(14170028894449352711)
XLA Ops:
  0.0 0.7 and_select_fusion
  0.7 0.8 and_select_fusion.1
  1.5 0.7 and_select_fusion.7
  2.3 0.1 copy.8.where
  2.4 0.0 copy-start.1
  2.4 0.9 copy-done.1
  3.3 0.0 copy-start.2
  3.3 0.9 copy-done.2
  4.3 59.0 %gather_factors.1 = (bf16[2,4,8,512,256]{4,3,2,1,0:T(8,128)(2,1)}, f32[256,256]{1,0:T(8,128)S(1)}) custom-call(bf16[512,256]{1,0:T(8,128)(2,1)S(1)} %copy-done.1, bf16[512,256]{1,0:T(8,128)(2,1)S(1)} %copy-done.2), custom_call_target="tpu_custom_call" | custom-call | tf_op jit(solution)/shard_map/gather_factors/pallas_call | solution.py:213
  63.2 0.0 copy-start
  63.3 4.6 %copy-done = bf16[24,64,4096]{2,1,0:T(8,128)(2,1)S(1)} copy-done((bf16[24,64,4096]{2,1,0:T(8,128)(2,1)S(1)}, bf16[24,64,4096]{2,1,0:T(8,128)(2,1)}, u32[]{:S(2)}) %copy-start) | copy-done | bytes 12582936
  67.8 21.1 %block_sums.1 = f32[16,64,256]{2,1,0:T(8,128)S(1)} custom-call(s32[24,7]{1,0:T(8,128)S(1)} %copy.8.where, bf16[24,64,4096]{2,1,0:T(8,128)(2,1)S(1)} %copy-done, bf16[2,4,8,512,256]{4,3,2,1,0:T(8,128)(2,1)} %get-tuple-element.7.b_ref.c_ref, bf16[2,4,8,512,256]{4,3,2,1,0:T(8,128)(2,1)} %get-tuple-element.7.b_ref.c_ref), custom_call_target="tpu_custom_call" | custom-call | tf_op jit(solution)/shard_map/block_sums/pallas_call | solution.py:283
  88.9 33.8 %owner_rows.1 = f32[128,256]{1,0:T(8,128)S(1)} custom-call(f32[4,2,128,256]{3,2,1,0:T(8,128)S(1)} %bitcast.1, f32[256,256]{1,0:T(8,128)S(1)} %get-tuple-element.8.nm), custom_call_target="tpu_custom_call" | custom-call | tf_op jit(solution)/shard_map/owner_rows/pallas_call | solution.py:323
  122.8 0.7 copy.10
  (2 shorter events, 0.0 us)
Async XLA Ops:
  2.4 1.0 copy-start.1
  3.3 0.9 copy-start.2
  63.2 4.6 %copy-start = (bf16[24,64,4096]{2,1,0:T(8,128)(2,1)S(1)}, bf16[24,64,4096]{2,1,0:T(8,128)(2,1)}, u32[]{:S(2)}) copy-start(bf16[24,64,4096]{2,1,0:T(8,128)(2,1)} %v_ref.1) | copy-start | bytes 37748740

commit v2 on v1

v2 whole, which is shorter than its diff:
```python
import functools
import heapq

import jax
import jax.numpy as jnp
from jax import lax
from jax.experimental import pallas as pl
from jax.experimental.pallas import tpu as pltpu
from jax.sharding import PartitionSpec as P

MESH = pl.DeviceIdType.MESH
HI = lax.Precision.HIGHEST
BS, R = 64, 256
NB, GROUP, LANES = 64, 8, 128
SHARD, G = 512, 16
Q = 48
Z_AT, Z_ROWS = 4 * Q, 176
Y_AT, Y_ROWS = 4 * Q + 176, 144


RANK = (
    60, 25, 53, 36, 4, 44, 5, 89, 1, 51, 76, 24, 46, 9, 2, 95, 61, 74, 78, 49, 6, 7,
    91, 81, 32, 12, 33, 52, 27, 57, 31, 19, 88, 39, 58, 56, 73, 64, 10, 66, 72, 20, 85, 16,
    67, 41, 38, 93, 83, 47, 0, 18, 42, 82, 34, 90, 94, 22, 84, 70, 23, 29, 86, 26, 80, 59,
    17, 40, 63, 71, 28, 14, 54, 50, 79, 92, 43, 62, 3, 21, 55, 45, 30, 37, 13, 87, 69, 11,
    8, 75, 48, 77, 15, 35, 65, 68)
HOLD = (
    (2, 1), (10, 24), (11, 6), (15, 25), (18, 53), (24, 2), (27, 51), (28, 48), (30, 28), (33, 4),
    (34, 10), (35, 27), (37, 30), (39, 11), (42, 77), (43, 88), (47, 75), (50, 60), (55, 56), (57, 20),
    (58, 75), (59, 35), (61, 1), (62, 19), (63, 50), (64, 52), (66, 53), (67, 23), (68, 60), (69, 30),
    (70, 32), (71, 35), (72, 70), (73, 17), (74, 60), (77, 73), (78, 20), (79, 84), (82, 89), (84, 88),
    (85, 37), (86, 82), (88, 0), (89, 56), (90, 27), (91, 10), (92, 81), (93, 73), (95, 38))


def plan():
    msgs = []

    def add(name, dim, sign, src, dst, rows, deps, nbytes):
        landed = ("x", rows[1] + sign) + rows[2:] if dim == "x" else rows
        msgs.append(dict(name=name, dim=dim, sign=sign, src=src, dst=dst, rows=rows, landed=landed, deps=deps, bytes=nbytes))
        return len(msgs) - 1

    def half(sign, at, rows):
        first = (rows // 2 + 15) // 16 * 16
        return (at, first) if sign > 0 else (at + first, rows - first)

    def z_ring(tag, rows_of, pys, first_deps, count):
        ids = {}
        for d in (1, 2, 3, 4):
            for s in (1, -1):
                src = 3 + s * (d - 1)
                dst = 3 + s * d if d < 4 else 7
                rows = rows_of(None) if d < 4 else rows_of(s)
                deps = [ids[d - 1, s]] if d > 1 else list(first_deps)
                ids[d, s] = add((tag, d, s), "z", s, (pys, (src, 1)), (pys, (dst, 1)), rows, deps, count * rows[-1] * 512)
        return ids

    def at_pz(ids, pz):
        dz = pz - 3
        if dz == 0:
            return []
        return [ids[4, 1], ids[4, -1]] if dz == 4 else [ids[abs(dz), 1 if dz > 0 else -1]]

    def y_ring(tag, rows_of, pz, deps, count):
        ids = {}
        for t in (1, -1):
            rows = rows_of(None)
            ids[1, t] = add((tag, 1, t), "y", t, ((1, 1), pz), ((1 + t, 1), pz), rows, list(deps), count * rows[-1] * 512)
        for t in (1, -1):
            rows = rows_of(t)
            ids[2, t] = add((tag, 2, t), "y", t, ((1 + t, 1), pz), ((3, 1), pz), rows, [ids[1, t]], count * rows[-1] * 512)
        return ids

    def x_rows(dx, sign):
        return ("x", dx) + ((0, Q) if sign is None else half(sign, 0, Q))

    def fixed(at, rows):
        return lambda sign: ("r",) + ((at, rows) if sign is None else half(sign, at, rows))

    xz = z_ring("xz", lambda s: x_rows(0, s), (1, 1), [], 1)
    zz = z_ring("zz", fixed(Z_AT, Z_ROWS), (1, 1), [], 1)
    yy = y_ring("yy", fixed(Y_AT, Y_ROWS), (3, 1), [], 1)
    xy = y_ring("xy", lambda s: x_rows(0, s), (0, 8), list(xz.values()), 8)
    x_groups = [
        (1, (2, 3), [xz[1, 1], xz[1, -1]]),
        (1, (0, 2), [xz[2, -1], xz[3, -1]]),
        (1, (5, 3), [xz[2, 1], xz[3, 1], xz[4, 1], xz[4, -1]]),
        (2, (0, 8), [xy[1, 1]]), (0, (0, 8), [xy[1, -1]]), (3, (0, 8), [xy[2, 1], xy[2, -1]])]
    for py, pz, deps in x_groups:
        place = ((py, 1), pz)
        first = {}
        for u in (1, -1):
            rows = x_rows(0, None)
            first[u] = add(("xx", py, pz, 1, u), "x", u, place, place, rows, list(deps), pz[1] * Q * 512)
        for u in (1, -1):
            rows = x_rows(u, u)
            add(("xx", py, pz, 2, u), "x", u, place, place, rows, [first[u]], pz[1] * rows[-1] * 512)
    for pz in (3, 4, 2, 5, 1, 6, 0, 7):
        y_ring(("zy", pz), fixed(Z_AT, Z_ROWS), (pz, 1), at_pz(zz, pz), 1)
    z_ring("yzA", fixed(Y_AT, Y_ROWS), (0, 2), [yy[1, -1]], 2)
    z_ring("yzB", fixed(Y_AT, Y_ROWS), (2, 2), [yy[1, 1], yy[2, 1], yy[2, -1]], 2)
    late = {("zz", 2): [xz[2, 1], xz[2, -1]], ("zz", 3): [xz[3, 1], xz[3, -1]], ("yzA", 1): [xz[4, 1], xz[4, -1]],
            ("yzB", 1): [xz[4, 1], xz[4, -1]]}
    for m in msgs:
        m["deps"] += late.get(m["name"][:2], [])
        if m["name"][0] in (("zy", 5), ("zy", 1)) and m["name"][1] == 1:
            m["deps"] += list(xz.values())
    for i, other in HOLD:
        msgs[i]["deps"].append(other)
    return msgs


def order(msgs, rate=45e3, latency=1.5):
    free = {}
    got = set()
    started = set()
    heap = []
    t_end = {}

    def issue(now):
        for i in RANK:
            m = msgs[i]
            if i not in started and all(d in got for d in m["deps"]):
                started.add(i)
                link = (m["dim"], m["sign"])
                begin = max(now, free.get(link, 0.0))
                free[link] = begin + m["bytes"] / rate
                heapq.heappush(heap, (free[link] + latency, i))

    issue(0.0)
    seq = []
    while heap:
        t, i = heapq.heappop(heap)
        got.add(i)
        seq.append(i)
        t_end[i] = t
        issue(t)
    return seq, t_end, free


def sweep(m_ref, k, nb=NB, group=GROUP):
    n = m_ref.shape[0]
    at = k * nb
    tiles = n // LANES
    home, off = at // LANES, at % LANES
    r = m_ref[at:at + nb, :]
    panel = [m_ref[at:at + nb, t * LANES:(t + 1) * LANES] for t in range(tiles)]
    lane = lax.broadcasted_iota(jnp.int32, (nb, LANES), 1)
    row = lax.broadcasted_iota(jnp.int32, (nb, LANES), 0)

    def spread(v):
        return jnp.broadcast_to(v, (nb, LANES))

    for j0 in range(0, nb, group):
        cols = [spread(panel[home][:, off + j:off + j + 1]) for j in range(j0, j0 + group)]
        rows = [[p[j:j + 1, :] for p in panel] for j in range(j0, j0 + group)]
        for i in range(group):
            j = j0 + i
            inv = 1.0 / cols[i][j:j + 1, :]
            here = lane[:1] == off + j
            scaled = [rows[i][t] * inv for t in range(tiles)]
            scaled[home] = jnp.where(here, inv, scaled[home])
            for a in range(i + 1, group):
                f = cols[a][j:j + 1, :] * inv
                cols[a] = jnp.where(row == j, spread(f), cols[a] - cols[i] * f)
                g = cols[i][j0 + a:j0 + a + 1, :]
                cleared = [rows[a][t] if t != home else jnp.where(here, 0.0, rows[a][t]) for t in range(tiles)]
                rows[a] = [cleared[t] - g * scaled[t] for t in range(tiles)]
            for t in range(tiles):
                old = panel[t] if t != home else jnp.where(lane == off + j, 0.0, panel[t])
                panel[t] = jnp.where(row == j, spread(scaled[t]), old - cols[i] * scaled[t])
    inside = (lane >= off) & (lane < off + nb)
    w = [jnp.where(inside, -p, p) if t == home else p for t, p in enumerate(panel)]
    upd = lax.dot_general(r, jnp.concatenate(w, axis=1), (((0,), (0,)), ((), ())), precision=HI,
                          preferred_element_type=jnp.float32)
    big = lax.broadcasted_iota(jnp.int32, (1, n), 1)
    m_ref[...] = jnp.where((big >= at) & (big < at + nb), 0.0, m_ref[...]) - upd
    for t in range(tiles):
        m_ref[at:at + nb, t * LANES:(t + 1) * LANES] = w[t]


def kernel(msgs, seq, unroll, coords, b_hbm, c_hbm, v_hbm, out, both, g, gsib, m, v, sums, away, pair, near, parts,
           own_sem, send, recv, sib_send, sib_recv, gs, gr, v_sem, s1, r1, s2, r2):
    grp, wide = lax.axis_index("grp"), lax.axis_index("wide")
    x, core = grp // 2, grp % 2
    y, z = wide // 8, wide % 8
    sib = (grp + 1 - 2 * core, wide)
    count = v_hbm.shape[0]
    mine = both.at[core]

    def dev(dim, s):
        if dim == "x":
            return (((x + s + 4) % 4) * 2 + core, wide)
        if dim == "y":
            return (grp, ((y + s + 4) % 4) * 8 + z)
        return (grp, y * 8 + (z + s + 8) % 8)

    def row_slice(rows):
        if rows[0] == "r":
            return pl.ds(rows[1] // G, rows[2] // G)
        return pl.ds(((x - rows[1] + 4) % 4) * (Q // G) + rows[2] // G, rows[3] // G)

    def region(place, rows):
        (py, npy), (pz, npz) = place
        return mine.at[pl.ds(py, npy), pl.ds(pz, npz), row_slice(rows)]

    peers = [dev(d, s) for d in "xyz" for s in (1, -1)] + [dev("x", 2), sib]
    bar = pltpu.get_barrier_semaphore()
    for p in peers:
        pl.semaphore_signal(bar, inc=1, device_id=p, device_id_type=MESH)

    own_rows = [("x", 0, 0, Q), ("r", Z_AT, SHARD - Z_AT)]
    own_place = ((1, 1), (3, 1))
    for k, src in enumerate((b_hbm, c_hbm)):
        @pl.when(core == k)
        def _():
            for j, rows in enumerate(own_rows):
                pltpu.make_async_copy(src.at[row_slice(rows)], mine.at[1, 3, row_slice(rows)], own_sem.at[j]).start()
    for j, rows in enumerate(own_rows):
        pltpu.make_async_copy(b_hbm.at[row_slice(rows)], mine.at[1, 3, row_slice(rows)], own_sem.at[j]).wait()
    pl.semaphore_wait(bar, len(peers))

    def copy(i):
        q = msgs[i]
        return pltpu.make_async_remote_copy(
            src_ref=region(q["src"], q["rows"]), dst_ref=region(q["dst"], q["rows"]),
            send_sem=send.at[i], recv_sem=recv.at[i], device_id=dev(q["dim"], q["sign"]), device_id_type=MESH)

    def hand_over(place, rows):
        pltpu.make_async_remote_copy(
            src_ref=region(place, rows), dst_ref=region(place, rows),
            send_sem=sib_send, recv_sem=sib_recv, device_id=sib, device_id_type=MESH).start()

    def add_gram(place, rows):
        (py, npy), (pz, npz) = place
        f = both[core, pl.ds(py, npy), pl.ds(pz, npz), row_slice(rows)].reshape(-1, R)
        g[...] += lax.dot_general(f, f, (((0,), (0,)), ((), ())), preferred_element_type=jnp.float32)

    started, got = set(), set()

    def issue():
        for i in RANK:
            if i not in started and all(d in got for d in msgs[i]["deps"]):
                started.add(i)
                copy(i).start()

    def value_copy(n):
        return pltpu.make_async_copy(v_hbm.at[n], v.at[n], v_sem.at[n])

    issue()
    for rows in own_rows:
        hand_over(own_place, rows)

    g[...] = jnp.zeros_like(g)
    for rows in own_rows:
        add_gram(own_place, rows)
    for k, i in enumerate(seq):
        copy(i).wait_recv()
        got.add(i)
        issue()
        if k >= 16 and k % 3 == 1 and (k - 16) // 3 < count:
            value_copy((k - 16) // 3).start()
        hand_over(msgs[i]["dst"], msgs[i]["landed"])
        add_gram(msgs[i]["dst"], msgs[i]["landed"])
    swap = pltpu.make_async_remote_copy(src_ref=g, dst_ref=gsib, send_sem=gs, recv_sem=gr, device_id=sib, device_id_type=MESH)
    swap.start()
    for i in range(len(msgs)):
        copy(i).wait_send()
    theirs = pltpu.make_async_remote_copy(src_ref=mine, dst_ref=both.at[1 - core], send_sem=sib_send, recv_sem=sib_recv,
                                          device_id=sib, device_id_type=MESH)
    theirs.wait()

    chunk = 512
    per = chunk // BS

    def factor_rows(k, n):
        at = coords[k + 1, n]
        py, pz, first = (y - (at >> 6) + 5) & 3, (z - (at >> 3) + 11) & 7, (at & 7) * (BS // G)
        return jnp.concatenate([both[k, py, pz, first + i] for i in range(BS // G)], axis=0)

    @pl.loop(0, count // unroll)
    def _(step):
        for u in range(unroll):
            value_copy(step * unroll + u).wait()
        for u in range(unroll):
            n = step * unroll + u
            b = factor_rows(0, n)
            c = factor_rows(1, n).astype(jnp.float32)
            for q in range(BS // per):
                prod = lax.dot_general(v[n, :, q * chunk:(q + 1) * chunk], b, (((0,), (0,)), ((), ())),
                                       preferred_element_type=jnp.float32)
                sums[n, q * per:(q + 1) * per, :] = jnp.sum(prod.reshape(per, BS, R) * c[None], axis=1)

    def owned_by(to_core, to_x, half):
        row = (to_x * 2 + to_core) * 2 + half
        total = jnp.zeros((BS, R), jnp.float32)
        for n in range(count):
            at = coords[0, n]
            miss = jnp.abs((at >> 6) * 2 + (at & 1) - row)
            total = total + sums[n] * (1 - jnp.minimum(miss, 1)).astype(jnp.float32)
        return total

    for to_x in range(4):
        for half in range(2):
            away[to_x, half * BS:(half + 1) * BS, :] = owned_by(1 - core, to_x, half)
    pass_on = pltpu.make_async_remote_copy(src_ref=away, dst_ref=pair, send_sem=s1, recv_sem=r1, device_id=sib,
                                           device_id_type=MESH)
    pass_on.start()
    for to_x in range(4):
        for half in range(2):
            near[to_x, half * BS:(half + 1) * BS, :] = owned_by(core, to_x, half)
    swap.wait()
    m[...] = g[...] * gsib[...]
    sweep(m, 0)
    pass_on.wait()
    near[...] += pair[...]
    far = []
    for d in (2, 1, 3):
        far.append(pltpu.make_async_remote_copy(
            src_ref=near.at[(x + d) % 4], dst_ref=parts.at[d - 1], send_sem=s2.at[d - 1], recv_sem=r2.at[d - 1],
            device_id=dev("x", d), device_id_type=MESH))
        far[-1].start()
    for k in range(1, R // NB):
        sweep(m, k)
    for q in far:
        q.wait()
    rows = near[x] + parts[0] + parts[1] + parts[2]
    out[...] = -jnp.dot(rows, m[...], precision=HI, preferred_element_type=jnp.float32)


def local(block_coords, block_values, factor_b, factor_c):
    msgs = plan()
    seq = order(msgs)[0]
    n = len(msgs)
    count = block_values.shape[0]
    rows = 2 * BS
    hbm = pl.BlockSpec(memory_space=pltpu.HBM)
    dma = pltpu.SemaphoreType.DMA
    square = pltpu.VMEM((R, R), jnp.float32)
    four = pltpu.VMEM((4, rows, R), jnp.float32)
    return pl.pallas_call(
        functools.partial(kernel, msgs, seq, 3),
        out_shape=jax.ShapeDtypeStruct((rows, R), jnp.float32),
        in_specs=[pl.BlockSpec(memory_space=pltpu.SMEM), hbm, hbm, hbm],
        out_specs=pl.BlockSpec(memory_space=pltpu.VMEM),
        scratch_shapes=[
            pltpu.VMEM((2, 4, 8, SHARD // G, G, R), jnp.bfloat16), square, square, square,
            pltpu.VMEM(block_values.shape, jnp.bfloat16), pltpu.VMEM((count, BS, R), jnp.float32), four, four, four,
            pltpu.VMEM((3, rows, R), jnp.float32),
            dma((2,)), dma((n,)), dma((n,)), dma, dma, dma, dma, dma((count,)), dma, dma, dma((3,)), dma((3,))],
        compiler_params=pltpu.CompilerParams(collective_id=0, has_side_effects=True, vmem_limit_bytes=56 << 20),
        name="als_update",
    )(block_coords.T, factor_b.reshape(-1, G, R), factor_c.reshape(-1, G, R), block_values)


def solution(mesh):
    in_specs = (P(("grp", "wide"), None), P(("grp", "wide"), None, None), P("wide", None), P("wide", None))
    return jax.shard_map(local, mesh=mesh, in_specs=in_specs, out_specs=P(("grp", "wide"), None), check_vma=False)
```

time: 125 us -> 95 us (0.76); the launches traced: 123 us -> 94.9 us
  Pallas kernels: 114 us -> 93.3 us
  local copies, waits for them, and re-layouts: 7.24 us -> 1.57 us
  other arithmetic: 2.23 us -> 0 us
    pallas_call x3 -> x1, Pallas kernels: 114 us -> 93.3 us  [local(): pl.pallas_call(functools.partial(kernel, msgs, seq, 3), out_shape=jax.Sha...]
    unnamed x7 -> x1, local copies, waits for them, and re-layouts: 7.13 us -> 1.57 us
    select_n x4 -> x0, other arithmetic: 2.23 us -> none  [place(): return [(y - owner // 8 + 1) % 4, (z - owner % 8 + 3) % 8, rows % 8]]
where the time goes in v2:
time: 95 us; the launch traced here: 94.9 us
  Pallas kernels  93.3 us (98%)
  local copies, waits for them, and re-layouts  1.57 us (2%)
    pallas_call x1, Pallas kernels, local(): pl.pallas_call(functools.partial(kernel, msgs, seq, 3), out_shape=jax.Sha...  93.3 us

profile of v2, /device:TPU:1, one launch (start us, length us, event | category | flops | bytes accessed | tf_op | source)
XLA Modules:
  0.0 94.9 jit_solution(11673077569610344713)
XLA Ops:
  0.0 93.3 %als_update.1 = f32[128,256]{1,0:T(8,128)} custom-call(s32[3,24]{1,0:T(4,128)} %bitcast.5, bf16[32,16,256]{2,1,0:T(8,128)(2,1)} %bitcast.3, bf16[32,16,256]{2,1,0:T(8,128)(2,1)} %bitcast.4, bf16[24,64,4096]{2,1,0:T(8,128)(2,1)} %v_hbm.1), custom_call_target="tpu_custom_call" | custom-call | tf_op jit(solution)/shard_map/als_update/pallas_call | solution.py:341
  93.3 1.6 %copy.6 = f32[128,256]{1,0:T(8,128)} copy(f32[128,256]{1,0:T(8,128)} %als_update.1) | data formatting | bytes 262144

commit v3 on v2

--- a/solution.py
+++ b/solution.py
@@ -14,22 +14,21 @@
 NB, GROUP, LANES = 64, 8, 128
 SHARD, G = 512, 16
 Q = 48
-Z_AT, Z_ROWS = 4 * Q, 176
-Y_AT, Y_ROWS = 4 * Q + 176, 144
+Z_AT, Z_ROWS = 4 * Q, 160
+Y_AT, Y_ROWS = 4 * Q + 160, 160
 
 
 RANK = (
-    60, 25, 53, 36, 4, 44, 5, 89, 1, 51, 76, 24, 46, 9, 2, 95, 61, 74, 78, 49, 6, 7,
-    91, 81, 32, 12, 33, 52, 27, 57, 31, 19, 88, 39, 58, 56, 73, 64, 10, 66, 72, 20, 85, 16,
-    67, 41, 38, 93, 83, 47, 0, 18, 42, 82, 34, 90, 94, 22, 84, 70, 23, 29, 86, 26, 80, 59,
-    17, 40, 63, 71, 28, 14, 54, 50, 79, 92, 43, 62, 3, 21, 55, 45, 30, 37, 13, 87, 69, 11,
-    8, 75, 48, 77, 15, 35, 65, 68)
+    82, 6, 16, 93, 47, 53, 15, 18, 70, 80, 12, 75, 27, 21, 19, 30, 0, 33, 52, 83, 14, 5, 49, 50, 56, 35,
+    94, 20, 39, 84, 81, 7, 25, 72, 88, 4, 40, 74, 71, 87, 29, 34, 59, 31, 32, 76, 62, 58, 43, 37, 57, 92,
+    1, 85, 54, 26, 11, 60, 3, 17, 69, 28, 51, 61, 90, 67, 46, 24, 77, 65, 8, 23, 86, 63, 36, 64, 89, 38,
+    22, 10, 68, 9, 55, 13, 44, 48, 79, 73, 78, 41, 2, 45, 66, 95, 42, 91)
 HOLD = (
-    (2, 1), (10, 24), (11, 6), (15, 25), (18, 53), (24, 2), (27, 51), (28, 48), (30, 28), (33, 4),
-    (34, 10), (35, 27), (37, 30), (39, 11), (42, 77), (43, 88), (47, 75), (50, 60), (55, 56), (57, 20),
-    (58, 75), (59, 35), (61, 1), (62, 19), (63, 50), (64, 52), (66, 53), (67, 23), (68, 60), (69, 30),
-    (70, 32), (71, 35), (72, 70), (73, 17), (74, 60), (77, 73), (78, 20), (79, 84), (82, 89), (84, 88),
-    (85, 37), (86, 82), (88, 0), (89, 56), (90, 27), (91, 10), (92, 81), (93, 73), (95, 38))
+    (12, 52), (18, 17), (21, 13), (22, 61), (23, 5), (24, 17), (26, 58), (29, 9), (30, 6), (34, 49),
+    (35, 16), (38, 64), (39, 10), (42, 24), (43, 38), (44, 68), (45, 56), (47, 3), (50, 22), (52, 49),
+    (53, 17), (60, 51), (61, 49), (62, 72), (63, 52), (67, 22), (69, 73), (72, 30), (74, 12), (77, 10),
+    (78, 60), (79, 0), (81, 59), (82, 26), (84, 56), (85, 53), (86, 23), (88, 29), (89, 3), (92, 83),
+    (93, 60), (94, 64), (95, 81))
 
 
 def plan():
@@ -110,7 +109,7 @@
     return msgs
 
 
-def order(msgs, rate=45e3, latency=1.5):
+def order(msgs, rate=45e3, latency=2.5):
     free = {}
     got = set()
     started = set()
@@ -264,8 +263,6 @@
         add_gram(msgs[i]["dst"], msgs[i]["landed"])
     swap = pltpu.make_async_remote_copy(src_ref=g, dst_ref=gsib, send_sem=gs, recv_sem=gr, device_id=sib, device_id_type=MESH)
     swap.start()
-    for i in range(len(msgs)):
-        copy(i).wait_send()
     theirs = pltpu.make_async_remote_copy(src_ref=mine, dst_ref=both.at[1 - core], send_sem=sib_send, recv_sem=sib_recv,
                                           device_id=sib, device_id_type=MESH)
     theirs.wait()
@@ -324,6 +321,8 @@
         sweep(m, k)
     for q in far:
         q.wait()
+    for i in range(len(msgs)):
+        copy(i).wait_send()
     rows = near[x] + parts[0] + parts[1] + parts[2]
     out[...] = -jnp.dot(rows, m[...], precision=HI, preferred_element_type=jnp.float32)
 
@@ -339,7 +338,7 @@
     square = pltpu.VMEM((R, R), jnp.float32)
     four = pltpu.VMEM((4, rows, R), jnp.float32)
     return pl.pallas_call(
-        functools.partial(kernel, msgs, seq, 3),
+        functools.partial(kernel, msgs, seq, 4),
         out_shape=jax.ShapeDtypeStruct((rows, R), jnp.float32),
         in_specs=[pl.BlockSpec(memory_space=pltpu.SMEM), hbm, hbm, hbm],
         out_specs=pl.BlockSpec(memory_space=pltpu.VMEM),

time: 95 us -> 93.1 us (0.980)
  Pallas kernels: 93.3 us -> 91.4 us
    pallas_call x1, Pallas kernels: 93.3 us -> 91.4 us  [local(): pl.pallas_call(functools.partial(kernel, msgs, seq, 4), out_shape=jax.Sha...]
where the time goes in v3:
time: 93.1 us; the launch traced here: 93 us
  Pallas kernels  91.4 us (98%)
  local copies, waits for them, and re-layouts  1.57 us (2%)
    pallas_call x1, Pallas kernels, local(): pl.pallas_call(functools.partial(kernel, msgs, seq, 4), out_shape=jax.Sha...  91.4 us

profile of v3, /device:TPU:1, one launch (start us, length us, event | category | flops | bytes accessed | tf_op | source)
XLA Modules:
  0.0 93.0 jit_solution(14321984773889290872)
XLA Ops:
  0.0 91.4 %als_update.1 = f32[128,256]{1,0:T(8,128)} custom-call(s32[3,24]{1,0:T(4,128)} %bitcast.5, bf16[32,16,256]{2,1,0:T(8,128)(2,1)} %bitcast.3, bf16[32,16,256]{2,1,0:T(8,128)(2,1)} %bitcast.4, bf16[24,64,4096]{2,1,0:T(8,128)(2,1)} %v_hbm.1), custom_call_target="tpu_custom_call" | custom-call | tf_op jit(solution)/shard_map/als_update/pallas_call | solution.py:340
  91.4 1.6 %copy.6 = f32[128,256]{1,0:T(8,128)} copy(f32[128,256]{1,0:T(8,128)} %als_update.1) | data formatting | bytes 262144
